TPU v7x, 512 devices: a whole 4x4x16 slice. The times are simulated.
512 devices in a mesh: section: 32 (over z, core), sp: 16 (over x, y).
Axes of the slice: x: 4, y: 4, z: 16, core: 2. Of those that a mesh axis runs over, the one named last changes fastest.
Arguments:
- query: bfloat16 [32, 2048, 8192], P('section', 'sp'), may hold values from -11 to 11
- keyval: bfloat16 [32, 2048, 2048], P('section', 'sp'), may hold values from -11 to 11
- cache: bfloat16 [32, 16, 256, 256], P('section', 'sp'), may hold values from -4 to 4, as said below
- offsets: int32 [32], P('section'), may hold values from 0 to 32767
- lengths: int32 [32], P('section'), may hold values from 1 to 256
Outputs:
- forwarded: bfloat16 [32, 2048, 8192], P('section', 'sp')
Inputs may be any that keep to these rules, and one draw needn't show every extreme that they name: `cache`: slot k holds key-value head k * 8 // 16; slots that hold the same head are equal.
All inputs are finite; a program needn't handle non-finite values.
Results may differ from a plain program's by a relative error of at most 0.0096.
Values may be sent and summed in bfloat16 or wider, within the bound.
A program may use at most 64 MiB of HBM per device.

v0:
```python
import math

import jax
import jax.numpy as jnp
from jax import lax
from jax.sharding import PartitionSpec as P

QUERY_HEADS = 64
KEY_VALUE_HEADS = 8
HEAD_SIZE = 128


ROPE_BASE = 500000.0


def passed_along(value, axis, steps):
    count = lax.axis_size(axis)
    pairs = [(source, (source + steps) % count) for source in range(count)]
    return lax.ppermute(value, axis, pairs)


def rotation_tables(positions, head_width):
    half_width = head_width // 2
    exponent = jnp.arange(half_width, dtype=jnp.float32) * (-2.0 / head_width)
    frequency = jnp.power(jnp.float32(ROPE_BASE), exponent)
    angle = positions.astype(jnp.float32)[:, None] * frequency[None, :]
    return (jnp.cos(angle), jnp.sin(angle))


def rotate_pair(value_entries, cosine, sine):
    half_width = value_entries.shape[-1] // 2
    first = value_entries[..., :half_width].astype(jnp.float32)
    second = value_entries[..., half_width:].astype(jnp.float32)
    cos_wide = cosine[:, None, :]
    sin_wide = sine[:, None, :]
    return jnp.concatenate(
        [first * cos_wide - second * sin_wide, second * cos_wide + first * sin_wide], axis=-1
    )


def attend_head(query_rows, key_rows, value_rows, cache_keys, cache_values, length, block_rows):
    scale = 1.0 / math.sqrt(query_rows.shape[-1])
    contract = (((1,), (1,)), ((), ()))
    cache_live = jnp.arange(cache_keys.shape[0], dtype=jnp.int32) < length
    results = []
    for block_index in range(query_rows.shape[0] // block_rows):
        first_row = block_index * block_rows
        key_reach = first_row + block_rows
        block_queries = query_rows[first_row:key_reach]
        cache_scores = (
            lax.dot_general(block_queries, cache_keys, contract, preferred_element_type=jnp.float32)
            * scale
        )
        own_scores = (
            lax.dot_general(
                block_queries, key_rows[:key_reach], contract, preferred_element_type=jnp.float32
            )
            * scale
        )
        cache_scores = jnp.where(cache_live[None, :], cache_scores, -jnp.inf)
        row_place = first_row + jnp.arange(block_rows, dtype=jnp.int32)
        causal = jnp.arange(key_reach, dtype=jnp.int32)[None, :] <= row_place[:, None]
        own_scores = jnp.where(causal, own_scores, -jnp.inf)
        row_top = jnp.maximum(jnp.max(cache_scores, axis=1), jnp.max(own_scores, axis=1))
        cache_weights = jnp.exp(cache_scores - row_top[:, None])
        own_weights = jnp.exp(own_scores - row_top[:, None])
        row_total = jnp.sum(cache_weights, axis=1) + jnp.sum(own_weights, axis=1)
        numerator = jnp.dot(
            cache_weights.astype(jnp.bfloat16), cache_values, preferred_element_type=jnp.float32
        )
        numerator = numerator + jnp.dot(
            own_weights.astype(jnp.bfloat16),
            value_rows[:key_reach],
            preferred_element_type=jnp.float32,
        )
        results.append((numerator / row_total[:, None]).astype(jnp.bfloat16))
    return jnp.concatenate(results, axis=0)


def on_device(query, keyval, cache, offsets, lengths):
    token_row_block = query.shape[1]
    group_total = lax.axis_size("sp")
    local_slots = cache.shape[1]
    head_copies = local_slots * group_total // KEY_VALUE_HEADS
    local_queries = query[0].reshape(token_row_block, QUERY_HEADS, HEAD_SIZE)
    head_queries = lax.all_to_all(local_queries, "sp", split_axis=1, concat_axis=0, tiled=True)
    span_rows = head_queries.shape[0]
    heads_here = head_queries.shape[1]
    local_head_pairs = keyval[0].reshape(token_row_block, KEY_VALUE_HEADS, 2 * HEAD_SIZE)
    broadened = jnp.repeat(local_head_pairs, head_copies, axis=1)
    head_pairs = lax.all_to_all(broadened, "sp", split_axis=1, concat_axis=0, tiled=True)
    positions = offsets[0] + jnp.arange(span_rows, dtype=jnp.int32)
    cosine, sine = rotation_tables(positions, HEAD_SIZE)
    rotated_keys = rotate_pair(head_pairs[..., :HEAD_SIZE], cosine, sine).astype(jnp.bfloat16)
    plain_values = head_pairs[..., HEAD_SIZE:]
    section_cache = cache[0]
    length = lengths[0]
    per_slot = heads_here // local_slots
    block_rows = min(512, span_rows)

    def head_step(head_index, finished):
        slot_index = head_index // per_slot
        picked = lax.dynamic_slice_in_dim(head_queries, head_index, 1, 1)
        rotated = rotate_pair(picked, cosine, sine)[:, 0].astype(jnp.bfloat16)
        slot_keys = lax.dynamic_index_in_dim(rotated_keys, slot_index, 1, False)
        slot_values = lax.dynamic_index_in_dim(plain_values, slot_index, 1, False)
        slot_cache = lax.dynamic_index_in_dim(section_cache, slot_index, 0, False)
        result = attend_head(
            rotated,
            slot_keys,
            slot_values,
            slot_cache[:, :HEAD_SIZE],
            slot_cache[:, HEAD_SIZE:],
            length,
            block_rows,
        )
        return lax.dynamic_update_slice_in_dim(finished, result[:, None, :], head_index, 1)

    finished = lax.fori_loop(
        0, heads_here, head_step, jnp.zeros((span_rows, heads_here, HEAD_SIZE), jnp.bfloat16)
    )
    passed = passed_along(finished, "section", 1)
    moved = lax.all_to_all(passed, "sp", split_axis=0, concat_axis=1, tiled=True).reshape(
        token_row_block, QUERY_HEADS * HEAD_SIZE
    )
    return moved.reshape(1, token_row_block, QUERY_HEADS * HEAD_SIZE)


def solution(mesh):
    return jax.shard_map(
        on_device,
        mesh=mesh,
        in_specs=(
            P("section", "sp", None),
            P("section", "sp", None),
            P("section", "sp", None, None),
            P("section"),
            P("section"),
        ),
        out_specs=P("section", "sp", None),
        check_vma=False,
    )
```

profile of v0, /device:TPU:224, one launch (start us, length us, event | category | flops | bytes accessed | tf_op | source)
XLA Modules:
  0.0 195.1 jit_solution(9252972371779005420)
XLA Ops:
  0.0 1.1 copy.33
  1.3 1.1 broadcast_in_dim.160
  2.3 7.0 %all-to-all-start.1 = ((bf16[128,16,256]{2,0,1:T(8,128)(2,1)}), bf16[128,16,256]{2,0,1:T(8,128)(2,1)S(1)}, u32[]{:S(2)}, u32[]{:S(2)}) async-start(bf16[128,16,256]{2,0,1:T(8,128)(2,1)} %bitcast.7), calls=%async_computation.1 | async-start | bytes 2097152 | tf_op jit(solution)/shard_map/all_to_all | solution.py:91
  9.4 4.1 %copy.21 = bf16[1,128,8192]{1,2,0:T(8,128)(2,1)} copy(bf16[1,128,8192]{2,1,0:T(8,128)(2,1)} %param.7) | data formatting | bytes 4194304 | tf_op args[0]
  13.5 13.7 %all-to-all-done.1 = bf16[128,16,256]{2,0,1:T(8,128)(2,1)S(1)} async-done(((bf16[128,16,256]{2,0,1:T(8,128)(2,1)}), bf16[128,16,256]{2,0,1:T(8,128)(2,1)S(1)}, u32[]{:S(2)}, u32[]{:S(2)}) %all-to-all-start.1) | async-done | bytes 1048608 | tf_op jit(solution)/shard_map/all_to_all | solution.py:91
  27.1 4.4 %all-to-all-start = ((bf16[128,64,128]{0,2,1:T(8,128)(2,1)}), bf16[128,64,128]{0,2,1:T(8,128)(2,1)}, u32[]{:S(2)}, u32[]{:S(2)}) async-start(bf16[128,64,128]{0,2,1:T(8,128)(2,1)} %bitcast.1), calls=%async_computation | async-start | bytes 4194304 | tf_op jit(solution)/shard_map/all_to_all | solution.py:86
  33.0 2.3 %fusion.117 = (bf16[2048,1,64]{0,2,1:T(8,128)(2,1)S(1)}, bf16[2048,1,64]{0,2,1:T(8,128)(2,1)S(1)}) fusion(bf16[2048,1,64]{0,2,1:T(8,128)(2,1)S(1)} %copy.32, bf16[2048,1,64]{0,2,1:T(8,128)(2,1)S(1)} %copy.31, f32[64]{0:T(128)S(1)} %multiply_power_fusion, f32[2048]{0:T(1024)S(1)} %add_convert_fusion), kind=kLoop, calls=%fused_computation.131 | loop fusion | flops 1441792 | bytes 1057024 | tf_op jit(solution)/shard_map/convert.2
  35.6 23.8 %all-to-all-done = bf16[128,64,128]{0,2,1:T(8,128)(2,1)} async-done(((bf16[128,64,128]{0,2,1:T(8,128)(2,1)}), bf16[128,64,128]{0,2,1:T(8,128)(2,1)}, u32[]{:S(2)}, u32[]{:S(2)}) %all-to-all-start) | async-done | bytes 2097184 | tf_op jit(solution)/shard_map/all_to_all | solution.py:86
  59.4 3.1 %copy.23 = bf16[16,128,4,128]{3,1,0,2:T(8,128)(2,1)S(1)} copy(bf16[16,128,4,128]{1,3,2,0:T(8,128)(2,1)} %bitcast.4) | data formatting | bytes 4194304 | tf_op jit(solution)/shard_map/all_to_all | solution.py:86
  62.5 66.6 %while.15 = (s32[]{:T(128)}, bf16[2048,4,128]{2,0,1:T(8,128)(2,1)}, s32[]{:T(128)}, bf16[2048,4,128]{2,0,1:T(8,128)(2,1)S(1)}, bf16[1,256,256]{2,1,0:T(8,128)(2,...) while((s32[]{:T(128)}, bf16[2048,4,128]{2,0,1:T(8,128)(2,1)}, ...), condition=%wide.region_17.18_spmd.clone.clone, body=%wide.region_0.17_spmd.clone.clone.sunk | while | flops 1641412352 | bytes 52968588 | solution.py:119
  62.5 4.9 %fusion.194 = (bf16[2048,1,64]{2,0,1:T(8,128)(2,1)S(1)}, bf16[2048,1,64]{2,0,1:T(8,128)(2,1)S(1)}) fusion(f32[64]{0:T(128)S(1)} %get-tuple-element.385, f32[2048]{0:T(1024)S(1)} %get-tuple-element.386, bf16[2048,4,128]{2,0,1:T(8,128)(2,1)S(1)} %get-tuple-element.381, s32[]{:T(128)} %get-tuple-element.366, s32[]{:T(128)S(6)} %add.237), kind=kLoop, calls=%fused_computation.51.clone.1 | loop fusion | flops 1441792 | bytes 1057032 | tf_op jit(solution)/shard_map/convert
  75.4 1.0 fusion.197
  77.5 0.8 fusion.201
  79.2 4.9 %fusion.194 = (bf16[2048,1,64]{2,0,1:T(8,128)(2,1)S(1)}, bf16[2048,1,64]{2,0,1:T(8,128)(2,1)S(1)}) fusion(f32[64]{0:T(128)S(1)} %get-tuple-element.385, f32[2048]{0:T(1024)S(1)} %get-tuple-element.386, bf16[2048,4,128]{2,0,1:T(8,128)(2,1)S(1)} %get-tuple-element.381, s32[]{:T(128)} %get-tuple-element.366, s32[]{:T(128)S(6)} %add.237), kind=kLoop, calls=%fused_computation.51.clone.1 | loop fusion | flops 1441792 | bytes 1057032 | tf_op jit(solution)/shard_map/convert
  92.1 1.0 fusion.197
  95.9 4.9 %fusion.194 = (bf16[2048,1,64]{2,0,1:T(8,128)(2,1)S(1)}, bf16[2048,1,64]{2,0,1:T(8,128)(2,1)S(1)}) fusion(f32[64]{0:T(128)S(1)} %get-tuple-element.385, f32[2048]{0:T(1024)S(1)} %get-tuple-element.386, bf16[2048,4,128]{2,0,1:T(8,128)(2,1)S(1)} %get-tuple-element.381, s32[]{:T(128)} %get-tuple-element.366, s32[]{:T(128)S(6)} %add.237), kind=kLoop, calls=%fused_computation.51.clone.1 | loop fusion | flops 1441792 | bytes 1057032 | tf_op jit(solution)/shard_map/convert
  108.7 1.0 fusion.197
  112.5 4.9 %fusion.194 = (bf16[2048,1,64]{2,0,1:T(8,128)(2,1)S(1)}, bf16[2048,1,64]{2,0,1:T(8,128)(2,1)S(1)}) fusion(f32[64]{0:T(128)S(1)} %get-tuple-element.385, f32[2048]{0:T(1024)S(1)} %get-tuple-element.386, bf16[2048,4,128]{2,0,1:T(8,128)(2,1)S(1)} %get-tuple-element.381, s32[]{:T(128)} %get-tuple-element.366, s32[]{:T(128)S(6)} %add.237), kind=kLoop, calls=%fused_computation.51.clone.1 | loop fusion | flops 1441792 | bytes 1057032 | tf_op jit(solution)/shard_map/convert
  125.4 1.0 fusion.197
  129.2 3.4 %copy.28 = bf16[2048,4,128]{2,1,0:T(4,128)(2,1)S(1)} copy(bf16[2048,4,128]{2,0,1:T(8,128)(2,1)} %get-tuple-element.159) | data formatting | bytes 4194304 | tf_op jit(solution)/shard_map/while | solution.py:119
  132.6 25.4 %collective-permute-done = bf16[2048,4,128]{2,1,0:T(4,128)(2,1)S(1)} collective-permute-done((bf16[2048,4,128]{2,1,0:T(4,128)(2,1)S(1)}, bf16[2048,4,128]{2,1,0:T(4,128)(2,1)S(1)}, u32[]{:S(2)}, u32[]{:S(2)}) %collective-permute-start) | collective-permute-done | bytes 2097184 | tf_op jit(solution)/shard_map/ppermute | solution.py:19
  158.1 33.1 %all_to_all.51 = bf16[2048,4,128]{2,1,0:T(4,128)(2,1)S(1)} all-to-all(bf16[2048,4,128]{2,1,0:T(4,128)(2,1)S(1)} %collective-permute-done), channel_id=1, replica_groups=mesh['section'=32,'sp'=16] {'sp'}, dimensions={0} | all-to-all | bytes 4194304 | tf_op jit(solution)/shard_map/all_to_all | solution.py:123
  191.1 1.2 copy.29
  192.3 2.8 %reshape_reshape.3 = bf16[1,128,8192]{2,1,0:T(8,128)(2,1)} reshape(bf16[128,16,4,128]{3,2,1,0:T(4,128)(2,1)S(1)} %copy.29) | data formatting | bytes 4194304 | tf_op jit(solution)/shard_map/reshape;reshape | solution.py:126
  (160 shorter events, 42.9 us)
Async XLA Ops:
  2.3 24.8 %all-to-all-start.1 = ((bf16[128,16,256]{2,0,1:T(8,128)(2,1)}), bf16[128,16,256]{2,0,1:T(8,128)(2,1)S(1)}, u32[]{:S(2)}, u32[]{:S(2)}) async-start(bf16[128,16,256]{2,0,1:T(8,128)(2,1)} %bitcast.7), calls=%async_computation.1 | async-start | bytes 2097152 | tf_op jit(solution)/shard_map/all_to_all | solution.py:91
  27.1 32.3 %all-to-all-start = ((bf16[128,64,128]{0,2,1:T(8,128)(2,1)}), bf16[128,64,128]{0,2,1:T(8,128)(2,1)}, u32[]{:S(2)}, u32[]{:S(2)}) async-start(bf16[128,64,128]{0,2,1:T(8,128)(2,1)} %bitcast.1), calls=%async_computation | async-start | bytes 4194304 | tf_op jit(solution)/shard_map/all_to_all | solution.py:86
  59.4 3.1 %copy-start = (bf16[1,1,256,256]{3,2,1,0:T(8,128)(2,1)S(1)}, bf16[1,1,256,256]{3,2,1,0:T(8,128)(2,1)}, u32[]{:S(2)}) copy-start(bf16[1,1,256,256]{3,2,1,0:T(8,128)(2,1)} %param.9) | copy-start | bytes 393220
  132.6 25.5 %collective-permute-start = (bf16[2048,4,128]{2,1,0:T(4,128)(2,1)S(1)}, bf16[2048,4,128]{2,1,0:T(4,128)(2,1)S(1)}, u32[]{:S(2)}, u32[]{:S(2)}) collective-permute-start(bf16[2048,4,128]{2,1,0:T(4,128)(2,1)S(1)} %copy.28), channel_id=1, source_target_pairs={{0,16},{16,32},{32,48},{48,64},{64,80},{80,96},{96,112},{112,128},... | collective-permute-start | bytes 6291464 | tf_op jit(solution)/shard_map/ppermute | solution.py:19
where the time goes:
time: 196 us; the launch traced here: 195 us
  waiting for transfers between devices  62.9 us (32%)
  other arithmetic  38.4 us (20%)
  blocking collectives  33.1 us (17%)
  matrix products  30.1 us (15%)
  local copies, waits for them, and re-layouts  17.8 us (9%)
  starting transfers between devices  11.5 us (6%)
    all_to_all x1, blocking collectives, on_device(): lax.all_to_all(passed, 'sp', split_axis=0, concat_axis=1, tiled=True)  33.1 us
    ppermute x1, waiting for transfers between devices, passed_along(): return lax.ppermute(value, axis, pairs)  25.4 us
    all_to_all x1, waiting for transfers between devices, on_device(): lax.all_to_all(local_queries, 'sp', split_axis=1, concat_axis=0, tiled=True)  23.8 us
    another operation x5, other arithmetic  22 us
    all_to_all x1, waiting for transfers between devices, on_device(): lax.all_to_all(broadened, 'sp', split_axis=1, concat_axis=0, tiled=True)  13.7 us
    dot_general x16, matrix products, attend_head(): lax.dot_general(block_queries, key_rows[:key_reach], contract, preferred_...  11.2 us
    reduce_sum x32, other arithmetic, attend_head(): row_total = jnp.sum(cache_weights, axis=1) + jnp.sum(own_weights, axis=1)  9.73 us
    dot_general x16, matrix products, attend_head(): jnp.dot(own_weights.astype(jnp.bfloat16), value_rows[:key_reach], preferr...  9.55 us
  transfers between devices with their start and end apart: 3, of which 3 were waited for; matrix products, arithmetic and copies ran while one was open for 4% of the time, Pallas kernels for 0%

commit v1 on v0

v1 whole, which is shorter than its diff:
```python
import functools
import math

import jax
import jax.numpy as jnp
from jax import lax
from jax.experimental import pallas as pl
from jax.experimental.pallas import tpu as pltpu
from jax.sharding import PartitionSpec as P

HEAD = 128
ROWS = 128
SIDE = 4
CACHE = 256
TILE = 512
SPAN = SIDE * SIDE * ROWS
ROPE_BASE = 500000.0
NEG = -1e30
SCALE = math.log2(math.e) / math.sqrt(HEAD)
MESH = pl.DeviceIdType.MESH
CONTRACT = (((1,), (1,)), ((), ()))
ORDER = (1, 3, 2)


def place(family, a, t):
    return SIDE * a + t if family == 0 else SIDE * t + a


def head_of(family, a):
    return 2 * a + 1 - a // 2 if family == 0 else 2 * a + a // 2


def kernel(
    sections,
    length_ref,
    query,
    keyval,
    cache,
    block_tab,
    row_tab,
    out,
    kvland,
    qland,
    cland,
    keys,
    values,
    qa,
    qb,
    sa,
    sb,
    ma,
    mb,
    obuf,
    kv1_send,
    kv2_send,
    kv_recv,
    q_send,
    q_recv,
    c_send,
    c_recv,
    o_send,
    o_recv,
):
    s = lax.axis_index("section")
    d = lax.axis_index("sp")
    x = d // SIDE
    y = d % SIDE
    head_at = (x, y)
    row_at = (y, x)
    after = lax.rem(s + 1, sections)
    before = lax.rem(s + sections - 1, sections)

    barrier = pltpu.get_barrier_semaphore()
    peers = []
    for k in range(1, SIDE):
        for f in range(2):
            peers.append((s, place(f, lax.rem(head_at[f] + k, SIDE), row_at[f])))
    for section in (after, before):
        peers.append((section, d))
        for k in range(1, SIDE):
            for f in range(2):
                peers.append((section, place(f, lax.rem(head_at[f] + k, SIDE), row_at[f])))
    for peer in peers:
        pl.semaphore_signal(barrier, inc=1, device_id=peer, device_id_type=MESH)
    pl.semaphore_wait(barrier, len(peers))

    def remote(source, target, send, recv, section, device):
        return pltpu.make_async_remote_copy(
            src_ref=source,
            dst_ref=target,
            send_sem=send,
            recv_sem=recv,
            device_id=(section, device),
            device_id_type=MESH,
        )

    def kv_part(f, a):
        return keyval.at[:, pl.ds(pl.multiple_of(head_of(f, a) * 256, 256), 256)]

    def q_part(f, a, half):
        return query.at[:, pl.ds(pl.multiple_of(head_of(f, a) * 1024 + half * 512, 512), 512)]

    def kv1(f, k):
        a = lax.rem(head_at[f] + k, SIDE)
        return remote(
            kv_part(f, a), kvland.at[f, d], kv1_send.at[f, k - 1], kv_recv.at[f, d], s, place(f, a, row_at[f])
        )

    def kv2(f, j, k):
        block = place(f, lax.rem(head_at[f] + j, SIDE), row_at[f])
        source = kv_part(f, head_at[f]) if j == 0 else kvland.at[f, block]
        target = place(f, head_at[f], lax.rem(row_at[f] + k, SIDE))
        return remote(source, kvland.at[f, block], kv2_send.at[f, j, k - 1], kv_recv.at[f, block], s, target)

    def q_copy(f, k, half):
        a = lax.rem(head_at[f] + k, SIDE)
        return remote(
            q_part(f, a, half),
            qland.at[f, head_at[f], half],
            q_send.at[f, k - 1, half],
            q_recv.at[f, head_at[f], half],
            s,
            place(f, a, row_at[f]),
        )

    def kv_own(f):
        return pltpu.make_async_copy(kv_part(f, head_at[f]), kvland.at[f, d], kv_recv.at[f, d])

    def q_own(f, half):
        return pltpu.make_async_copy(
            q_part(f, head_at[f], half), qland.at[f, head_at[f], half], q_recv.at[f, head_at[f], half]
        )

    def q_wait(f, a, half):
        pltpu.make_async_copy(q_part(f, a, half), qland.at[f, a, half], q_recv.at[f, a, half]).wait()

    def kv_wait(f, block):
        pltpu.make_async_copy(kv_part(f, 0), kvland.at[f, block], kv_recv.at[f, block]).wait()

    def cache_own(f):
        return pltpu.make_async_copy(cache, cland.at[f], c_recv.at[f])

    def cache_copy(f, k):
        if f == 0:
            target = SIDE * x + SIDE - 1 - y
        else:
            target = SIDE * lax.rem(x + k, SIDE) + y
        return remote(cache, cland.at[f], c_send.at[f, k - 1], c_recv.at[f], s, target)

    holds = (x // 2 != y // 2, x == y)

    def out_copy(f, a, half):
        column = head_of(f, head_at[f]) * 1024 + half * 512
        return remote(
            obuf.at[f, a, half],
            out.at[:, pl.ds(pl.multiple_of(column, 512), 512)],
            o_send.at[f, a, half],
            o_recv.at[f, head_at[f], half],
            after,
            place(f, a, row_at[f]),
        )

    def out_wait(f, a, half):
        column = head_of(f, a) * 1024 + half * 512
        pltpu.make_async_copy(
            obuf.at[f, a, half], out.at[:, pl.ds(pl.multiple_of(column, 512), 512)], o_recv.at[f, a, half]
        ).wait()

    for k in ORDER:
        for f in range(2):
            kv1(f, k).start()
    for k in ORDER:
        for f in range(2):
            kv2(f, 0, k).start()
    for f in range(2):
        kv_own(f).start()
        for half in range(2):
            q_own(f, half).start()

    for f, ks in ((0, (1,)), (1, ORDER)):

        @pl.when(holds[f])
        def _():
            cache_own(f).start()
            for k in ks:
                cache_copy(f, k).start()

    for half in range(2):
        for k in ORDER:
            q_copy(0, k, half).start()

    values[:, :, HEAD:] = jnp.ones((2, CACHE + SPAN, HEAD), jnp.bfloat16)

    for j in ORDER:
        kv_wait(0, place(0, lax.rem(head_at[0] + j, SIDE), row_at[0]))
        for k in ORDER:
            kv2(0, j, k).start()
    for j in ORDER:
        kv_wait(1, place(1, lax.rem(head_at[1] + j, SIDE), row_at[1]))
        for k in ORDER:
            kv2(1, j, k).start()
    for half in range(2):
        for k in ORDER:
            q_copy(1, k, half).start()
    for f in range(2):
        kv_wait(f, d)

    def tables(block):
        cos_block = block_tab[0, block]
        sin_block = block_tab[1, block]
        cos_signed = block_tab[2, block]
        sin_signed = block_tab[3, block]
        cos_row = row_tab[0]
        sin_row = row_tab[1]
        cosine = cos_block * cos_row - sin_block * sin_row
        sine = sin_signed * cos_row + cos_signed * sin_row
        return cosine, sine

    def rotate(entries, cosine, sine):
        wide = entries.astype(jnp.float32)
        return wide * cosine + pltpu.roll(wide, HEAD // 2, 1) * sine

    def take_block(f, block):
        cosine, sine = tables(block)
        first = pl.multiple_of(CACHE + block * ROWS, ROWS)
        keys[f, pl.ds(first, ROWS), :] = rotate(kvland[f, block, :, :HEAD], cosine, sine).astype(jnp.bfloat16)
        values[f, pl.ds(first, ROWS), :HEAD] = kvland[f, block, :, HEAD:]

    def take_cache(f):
        cache_own(f).wait()
        keys[f, :CACHE, :] = cland[f, :, :HEAD]
        values[f, :CACHE, :HEAD] = cland[f, :, HEAD:]

    def take_query(f, a, half, target):
        q_wait(f, a, half)
        cosine, sine = tables(place(f, a, row_at[f]))
        for h in range(TILE // ROWS):
            head = qland[f, a, half, :, h * HEAD : (h + 1) * HEAD]
            target[h * ROWS : (h + 1) * ROWS, :] = (rotate(head, cosine, sine) * SCALE).astype(jnp.bfloat16)

    length = length_ref[0]

    def score(f, q_ref, reach, shift, s_ref, m_ref):
        q = q_ref[...]
        column = lax.broadcasted_iota(jnp.int32, (1, CACHE), 1)
        part = lax.dot_general(q, keys[f, :CACHE, :], CONTRACT, preferred_element_type=jnp.float32)
        part = jnp.where(column < length, part, NEG)
        s_ref[:, :CACHE] = part
        top = jnp.maximum(part[:, :128], part[:, 128:])
        if reach > 512:
            part = lax.dot_general(
                q, keys[f, CACHE : reach - 256, :], CONTRACT, preferred_element_type=jnp.float32
            )
            s_ref[:, CACHE : reach - 256] = part
            for c in range(0, reach - 512, 128):
                top = jnp.maximum(top, part[:, c : c + 128])
        part = lax.dot_general(
            q, keys[f, reach - 256 : reach + 256, :], CONTRACT, preferred_element_type=jnp.float32
        )
        column = lax.broadcasted_iota(jnp.int32, (1, 512), 1)
        row = lax.rem(lax.broadcasted_iota(jnp.int32, (TILE, 1), 0), ROWS) + shift
        part = jnp.where(column <= row, part, NEG)
        s_ref[:, reach - 256 : reach + 256] = part
        for c in range(0, 512, 128):
            top = jnp.maximum(top, part[:, c : c + 128])
        m_ref[...] = jnp.broadcast_to(jnp.max(top, axis=1, keepdims=True), (TILE, 128))

    def combine(f, a, half, reach, s_ref, m_ref):
        width = reach + CACHE
        top = jnp.concatenate([m_ref[...]] * (width // 128), axis=1)
        probs = jnp.exp2(s_ref[:, :width] - top).astype(jnp.bfloat16)
        mixed = jnp.dot(probs, values[f, :width, :], preferred_element_type=jnp.float32)
        result = (mixed[:, :HEAD] / mixed[:, HEAD:]).astype(jnp.bfloat16)
        for h in range(TILE // ROWS):
            obuf[f, a, half, :, h * HEAD : (h + 1) * HEAD] = result[h * ROWS : (h + 1) * ROWS, :]

    def prepare(i):
        for k in ORDER:
            kv_wait(0, place(0, i, lax.rem(row_at[0] + k, SIDE)))
        for j in range(SIDE):
            take_block(0, SIDE * i + j)

    shift = row_at[0] * ROWS
    take_cache(0)
    prepare(0)
    take_query(0, 0, 0, qa)
    score(0, qa, 512, shift, sa, ma)
    for i in range(SIDE):
        reach = 512 * (i + 1)
        take_query(0, i, 1, qb)
        score(0, qb, reach, shift, sb, mb)
        combine(0, i, 0, reach, sa, ma)
        if i > 0:
            out_copy(0, i - 1, 1).start()
        if i < SIDE - 1:
            prepare(i + 1)
            take_query(0, i + 1, 0, qa)
            score(0, qa, reach + 512, shift, sa, ma)
        combine(0, i, 1, reach, sb, mb)
        out_copy(0, i, 0).start()

    take_cache(1)
    for k in ORDER:

        def wait_block(a, carry, k=k):
            kv_wait(1, place(1, a, lax.rem(row_at[1] + k, SIDE)))
            return carry

        lax.fori_loop(0, SIDE, wait_block, 0)

    def take_one(block, carry):
        take_block(1, block)
        return carry

    lax.fori_loop(0, SIDE * SIDE, take_one, 0)
    out_copy(0, SIDE - 1, 1).start()

    def run(reach):
        take_query(1, 0, 0, qa)
        score(1, qa, reach, 0, sa, ma)

        def unit(a, carry):
            take_query(1, a, 1, qb)
            score(1, qb, reach, a * ROWS, sb, mb)
            combine(1, a, 0, reach, sa, ma)

            @pl.when(a > 0)
            def _():
                out_copy(1, a - 1, 1).start()

            @pl.when(a < SIDE - 1)
            def _():
                take_query(1, a + 1, 0, qa)

            score(1, qa, reach, (a + 1) * ROWS, sa, ma)
            combine(1, a, 1, reach, sb, mb)
            out_copy(1, a, 0).start()
            return carry

        lax.fori_loop(0, SIDE, unit, 0)

    for t in range(SIDE):

        @pl.when(row_at[1] == t)
        def _(t=t):
            run(512 * (t + 1))

    out_copy(1, SIDE - 1, 1).start()

    for f in range(2):
        for k in ORDER:
            kv1(f, k).wait_send()
            for j in range(SIDE):
                kv2(f, j, k).wait_send()
            for half in range(2):
                q_copy(f, k, half).wait_send()
    for f, ks in ((0, (1,)), (1, ORDER)):

        @pl.when(holds[f])
        def _():
            for k in ks:
                cache_copy(f, k).wait_send()

    for f in range(2):
        for a in range(SIDE):
            for half in range(2):
                out_copy(f, a, half).wait_send()
                out_wait(f, a, half)


def angles(positions):
    exponent = jnp.arange(HEAD // 2, dtype=jnp.float32) * (-2.0 / HEAD)
    frequency = jnp.power(jnp.float32(ROPE_BASE), exponent)
    angle = positions.astype(jnp.float32)[:, None] * frequency[None, :]
    return jnp.cos(angle), jnp.sin(angle)


def on_device(query, keyval, cache, offsets, lengths):
    sections = lax.axis_size("section")
    blocks = offsets[0] + ROWS * jnp.arange(SIDE * SIDE, dtype=jnp.int32)
    cos_block, sin_block = angles(blocks)
    cos_row, sin_row = angles(jnp.arange(ROWS, dtype=jnp.int32))
    block_tab = jnp.stack(
        [
            jnp.concatenate([cos_block, cos_block], axis=1),
            jnp.concatenate([sin_block, sin_block], axis=1),
            jnp.concatenate([-cos_block, cos_block], axis=1),
            jnp.concatenate([-sin_block, sin_block], axis=1),
        ]
    )[:, :, None, :]
    row_tab = jnp.stack(
        [
            jnp.concatenate([cos_row, cos_row], axis=1),
            jnp.concatenate([sin_row, sin_row], axis=1),
        ]
    )
    bf16 = jnp.bfloat16
    anywhere = pl.BlockSpec(memory_space=pl.ANY)
    vmem = pl.BlockSpec(memory_space=pltpu.VMEM)
    result = pl.pallas_call(
        functools.partial(kernel, sections),
        out_shape=jax.ShapeDtypeStruct((ROWS, 64 * HEAD), bf16),
        in_specs=[pl.BlockSpec(memory_space=pltpu.SMEM), anywhere, anywhere, anywhere, vmem, vmem],
        out_specs=anywhere,
        scratch_shapes=[
            pltpu.VMEM((2, SIDE * SIDE, ROWS, 2 * HEAD), bf16),
            pltpu.VMEM((2, SIDE, 2, ROWS, TILE), bf16),
            pltpu.VMEM((2, CACHE, 2 * HEAD), bf16),
            pltpu.VMEM((2, CACHE + SPAN, HEAD), bf16),
            pltpu.VMEM((2, CACHE + SPAN, 2 * HEAD), bf16),
            pltpu.VMEM((TILE, HEAD), bf16),
            pltpu.VMEM((TILE, HEAD), bf16),
            pltpu.VMEM((TILE, CACHE + SPAN), jnp.float32),
            pltpu.VMEM((TILE, CACHE + SPAN), jnp.float32),
            pltpu.VMEM((TILE, 128), jnp.float32),
            pltpu.VMEM((TILE, 128), jnp.float32),
            pltpu.VMEM((2, SIDE, 2, ROWS, TILE), bf16),
            pltpu.SemaphoreType.DMA((2, 3)),
            pltpu.SemaphoreType.DMA((2, SIDE, 3)),
            pltpu.SemaphoreType.DMA((2, SIDE * SIDE)),
            pltpu.SemaphoreType.DMA((2, 3, 2)),
            pltpu.SemaphoreType.DMA((2, SIDE, 2)),
            pltpu.SemaphoreType.DMA((2, 3)),
            pltpu.SemaphoreType.DMA((2,)),
            pltpu.SemaphoreType.DMA((2, SIDE, 2)),
            pltpu.SemaphoreType.DMA((2, SIDE, 2)),
        ],
        compiler_params=pltpu.CompilerParams(
            collective_id=0, has_side_effects=True, vmem_limit_bytes=48 << 20
        ),
    )(lengths, query[0], keyval[0], cache[0, 0], block_tab, row_tab)
    return result[None]


def solution(mesh):
    return jax.shard_map(
        on_device,
        mesh=mesh,
        in_specs=(
            P("section", "sp", None),
            P("section", "sp", None),
            P("section", "sp", None, None),
            P("section"),
            P("section"),
        ),
        out_specs=P("section", "sp", None),
        check_vma=False,
    )
```

time: 196 us -> 79.6 us (0.41)
  the two profiles are of different devices: /device:TPU:224 before, /device:TPU:30 now
where the time goes in v1:
time: 79.6 us; the launch traced here: 79.4 us
  Pallas kernels  72.6 us (91%)
  local copies, waits for them, and re-layouts  4.85 us (6%)
  between operations  1.36 us (2%)
    pallas_call x1, Pallas kernels, on_device(): pl.pallas_call(functools.partial(kernel, sections), out_shape=jax.ShapeDt...  72.6 us
    unnamed x7, local copies, waits for them, and re-layouts  4.85 us

profile of v1, /device:TPU:30, one launch (start us, length us, event | category | flops | bytes accessed | tf_op | source)
XLA Modules:
  0.0 79.4 jit_solution(5932374053500920813)
XLA Ops:
  1.3 0.1 multiply_cosine_fusion.1
  1.5 0.1 maximum_bitcast_fusion.2
  1.5 0.3 multiply_cosine_fusion
  1.9 0.1 maximum_bitcast_fusion
  2.0 0.0 copy-start
  2.0 1.6 %copy-done = bf16[1,128,8192]{2,1,0:T(8,128)(2,1)S(1)} copy-done((bf16[1,128,8192]{2,1,0:T(8,128)(2,1)S(1)}, bf16[1,128,8192]{2,1,0:T(8,128)(2,1)}, u32[]{:S(2)}) %copy-start) | copy-done | bytes 2097176
  3.6 0.0 copy-start.1
  3.6 1.0 %copy-done.1 = bf16[1,128,2048]{2,1,0:T(8,128)(2,1)S(1)} copy-done((bf16[1,128,2048]{2,1,0:T(8,128)(2,1)S(1)}, bf16[1,128,2048]{2,1,0:T(8,128)(2,1)}, u32[]{:S(2)}) %copy-start.1) | copy-done | bytes 524312
  4.6 0.0 copy-start.2
  4.6 0.9 %copy-done.2 = bf16[1,1,256,256]{3,2,1,0:T(8,128)(2,1)S(1)} copy-done((bf16[1,1,256,256]{3,2,1,0:T(8,128)(2,1)S(1)}, bf16[1,1,256,256]{3,2,1,0:T(8,128)(2,1)}, u32[]{:S(2)}) %copy-start.2) | copy-done | bytes 131096
  5.5 72.6 %shard_map.55 = bf16[128,8192]{1,0:T(8,128)(2,1)S(1)} custom-call(s32[1]{0:T(128)S(6)} %copy.8.length_ref, bf16[128,8192]{1,0:T(8,128)(2,1)S(1)} %bitcast.20, bf16[128,2048]{1,0:T(8,128)(2,1)S(1)} %bitcast.21, bf16[256,256]{1,0:T(8,128)(2,1)S(1)} %bitcast.22, f32[4,16,1,128]{3,2,1,0:T(1,128)S(1)} %bitcast.23, f32[2,128,128]{2,1,0:T(8,128)S(1)} %pad_maximum_fusion.row_tab), custom_call_target="tpu_custom_call" | custom-call | tf_op jit(solution)/shard_map/pallas_call | solution.py:400
  78.1 1.3 %copy.9 = bf16[1,128,8192]{2,1,0:T(8,128)(2,1)} copy(bf16[1,128,8192]{2,1,0:T(8,128)(2,1)S(1)} %bitcast.19) | data formatting | bytes 4194304
  (5 shorter events, 0.0 us)
Async XLA Ops:
  2.0 1.6 %copy-start = (bf16[1,128,8192]{2,1,0:T(8,128)(2,1)S(1)}, bf16[1,128,8192]{2,1,0:T(8,128)(2,1)}, u32[]{:S(2)}) copy-start(bf16[1,128,8192]{2,1,0:T(8,128)(2,1)} %param.5) | copy-start | bytes 6291460
  3.6 1.0 %copy-start.1 = (bf16[1,128,2048]{2,1,0:T(8,128)(2,1)S(1)}, bf16[1,128,2048]{2,1,0:T(8,128)(2,1)}, u32[]{:S(2)}) copy-start(bf16[1,128,2048]{2,1,0:T(8,128)(2,1)} %param.6) | copy-start | bytes 1572868
  4.6 0.9 %copy-start.2 = (bf16[1,1,256,256]{3,2,1,0:T(8,128)(2,1)S(1)}, bf16[1,1,256,256]{3,2,1,0:T(8,128)(2,1)}, u32[]{:S(2)}) copy-start(bf16[1,1,256,256]{3,2,1,0:T(8,128)(2,1)} %param.7) | copy-start | bytes 393220

commit v2 on v1

--- a/solution.py
+++ b/solution.py
@@ -166,43 +166,57 @@
             obuf.at[f, a, half], out.at[:, pl.ds(pl.multiple_of(column, 512), 512)], o_recv.at[f, a, half]
         ).wait()
 
+    def gather(f, j, act):
+        for k in ORDER:
+            if f == 0:
+                act(kv2(f, j, k))
+            else:
+
+                @pl.when(row_at[f] + k < SIDE)
+                def _(k=k):
+                    act(kv2(f, j, k))
+
+    def start(copy):
+        copy.start()
+
     for k in ORDER:
-        for f in range(2):
-            kv1(f, k).start()
-    for k in ORDER:
-        for f in range(2):
-            kv2(f, 0, k).start()
-    for f in range(2):
+        kv1(1, k).start()
+    gather(1, 0, start)
+    for half in range(2):
+        for k in (3, 1, 2):
+            q_copy(1, k, half).start()
+    for f in (1, 0):
         kv_own(f).start()
         for half in range(2):
             q_own(f, half).start()
 
-    for f, ks in ((0, (1,)), (1, ORDER)):
-
-        @pl.when(holds[f])
-        def _():
-            cache_own(f).start()
-            for k in ks:
-                cache_copy(f, k).start()
-
+    @pl.when(holds[1])
+    def _():
+        cache_own(1).start()
+        for k in ORDER:
+            cache_copy(1, k).start()
+
+    values[:, :, HEAD:] = jnp.ones((2, CACHE + SPAN, HEAD), jnp.bfloat16)
+
+    def forward(f):
+        for j in ORDER:
+            kv_wait(f, place(f, lax.rem(head_at[f] + j, SIDE), row_at[f]))
+            gather(f, j, start)
+
+    forward(1)
+    for k in ORDER:
+        kv1(0, k).start()
+    gather(0, 0, start)
     for half in range(2):
-        for k in ORDER:
+        for k in (3, 1, 2):
             q_copy(0, k, half).start()
 
-    values[:, :, HEAD:] = jnp.ones((2, CACHE + SPAN, HEAD), jnp.bfloat16)
-
-    for j in ORDER:
-        kv_wait(0, place(0, lax.rem(head_at[0] + j, SIDE), row_at[0]))
-        for k in ORDER:
-            kv2(0, j, k).start()
-    for j in ORDER:
-        kv_wait(1, place(1, lax.rem(head_at[1] + j, SIDE), row_at[1]))
-        for k in ORDER:
-            kv2(1, j, k).start()
-    for half in range(2):
-        for k in ORDER:
-            q_copy(1, k, half).start()
-    for f in range(2):
+    @pl.when(holds[0])
+    def _():
+        cache_own(0).start()
+        cache_copy(0, 1).start()
+
+    for f in (1, 0):
         kv_wait(f, d)
 
     def tables(block):
@@ -274,67 +288,61 @@
         for h in range(TILE // ROWS):
             obuf[f, a, half, :, h * HEAD : (h + 1) * HEAD] = result[h * ROWS : (h + 1) * ROWS, :]
 
-    def prepare(i):
-        for k in ORDER:
-            kv_wait(0, place(0, i, lax.rem(row_at[0] + k, SIDE)))
-        for j in range(SIDE):
-            take_block(0, SIDE * i + j)
-
-    shift = row_at[0] * ROWS
-    take_cache(0)
-    prepare(0)
-    take_query(0, 0, 0, qa)
-    score(0, qa, 512, shift, sa, ma)
-    for i in range(SIDE):
-        reach = 512 * (i + 1)
-        take_query(0, i, 1, qb)
-        score(0, qb, reach, shift, sb, mb)
-        combine(0, i, 0, reach, sa, ma)
-        if i > 0:
-            out_copy(0, i - 1, 1).start()
-        if i < SIDE - 1:
-            prepare(i + 1)
-            take_query(0, i + 1, 0, qa)
-            score(0, qa, reach + 512, shift, sa, ma)
-        combine(0, i, 1, reach, sb, mb)
-        out_copy(0, i, 0).start()
+    def take_column(k):
+        def one(a, carry):
+            block = place(1, a, lax.rem(row_at[1] + k, SIDE))
+            if k:
+                kv_wait(1, block)
+            take_block(1, block)
+            return carry
+
+        lax.fori_loop(0, SIDE, one, 0)
+
+    take_column(0)
+    for k in ORDER:
+
+        @pl.when(row_at[1] + k >= SIDE)
+        def _(k=k):
+            take_column(k)
 
     take_cache(1)
-    for k in ORDER:
-
-        def wait_block(a, carry, k=k):
-            kv_wait(1, place(1, a, lax.rem(row_at[1] + k, SIDE)))
-            return carry
-
-        lax.fori_loop(0, SIDE, wait_block, 0)
-
-    def take_one(block, carry):
-        take_block(1, block)
-        return carry
-
-    lax.fori_loop(0, SIDE * SIDE, take_one, 0)
-    out_copy(0, SIDE - 1, 1).start()
+
+    def turn(f, n):
+        n = jnp.int32(n)
+        step = n + (n == 2).astype(jnp.int32) - (n == 3).astype(jnp.int32)
+        return lax.rem(head_at[f] + step, SIDE)
 
     def run(reach):
-        take_query(1, 0, 0, qa)
-        score(1, qa, reach, 0, sa, ma)
-
-        def unit(a, carry):
-            take_query(1, a, 1, qb)
-            score(1, qb, reach, a * ROWS, sb, mb)
-            combine(1, a, 0, reach, sa, ma)
-
-            @pl.when(a > 0)
+        def at(n):
+            return turn(1, n)
+
+        take_query(1, at(0), 0, qa)
+        score(1, qa, reach, at(0) * ROWS, sa, ma)
+
+        def unit(n, carry):
+            take_query(1, at(n), 1, qb)
+            score(1, qb, reach, at(n) * ROWS, sb, mb)
+            combine(1, at(n), 0, reach, sa, ma)
+
+            @pl.when(n == 0)
             def _():
-                out_copy(1, a - 1, 1).start()
-
-            @pl.when(a < SIDE - 1)
+                forward(0)
+
+            @pl.when(n > 0)
             def _():
-                take_query(1, a + 1, 0, qa)
-
-            score(1, qa, reach, (a + 1) * ROWS, sa, ma)
-            combine(1, a, 1, reach, sb, mb)
-            out_copy(1, a, 0).start()
+                out_copy(1, at(n - 1), 1).start()
+
+            @pl.when(n < SIDE - 1)
+            def _():
+                take_query(1, at(n + 1), 0, qa)
+                score(1, qa, reach, at(n + 1) * ROWS, sa, ma)
+                combine(1, at(n), 1, reach, sb, mb)
+
+            @pl.when(n == SIDE - 1)
+            def _():
+                combine(1, at(n), 1, reach, sb, mb)
+
+            out_copy(1, at(n), 0).start()
             return carry
 
         lax.fori_loop(0, SIDE, unit, 0)
@@ -345,19 +353,78 @@
         def _(t=t):
             run(512 * (t + 1))
 
-    out_copy(1, SIDE - 1, 1).start()
+    shift = row_at[0] * ROWS
+    take_cache(0)
+
+    def take_piece(a, carry):
+        for k in ORDER:
+            kv_wait(0, place(0, a, lax.rem(row_at[0] + k, SIDE)))
+        for t in range(SIDE):
+            take_block(0, place(0, a, t))
+        return carry
+
+    lax.fori_loop(0, SIDE, take_piece, 0)
+    take_query(0, lax.rem(x + 1, SIDE), 0, qa)
+    for i in range(SIDE):
+
+        @pl.when(lax.rem(x + 1, SIDE) == i)
+        def _(i=i):
+            score(0, qa, 512 * (i + 1), shift, sa, ma)
+
+    out_copy(1, turn(1, jnp.int32(3)), 1).start()
+
+    def unit0(n, carry):
+        now = lax.rem(x + 1 + n, SIDE)
+        then = lax.rem(now + 1, SIDE)
+        take_query(0, now, 1, qb)
+
+        @pl.when(n < SIDE - 1)
+        def _():
+            take_query(0, then, 0, qa)
+
+        for i in range(SIDE):
+
+            @pl.when(now == i)
+            def _(i=i):
+                reach = 512 * (i + 1)
+                score(0, qb, reach, shift, sb, mb)
+                combine(0, i, 0, reach, sa, ma)
+
+        @pl.when(n > 0)
+        def _():
+            out_copy(0, lax.rem(now + SIDE - 1, SIDE), 1).start()
+
+        for i in range(SIDE):
+
+            @pl.when(jnp.logical_and(now == i, n < SIDE - 1))
+            def _(i=i):
+                score(0, qa, 512 * ((i + 1) % SIDE + 1), shift, sa, ma)
+                combine(0, i, 1, 512 * (i + 1), sb, mb)
+
+            @pl.when(jnp.logical_and(now == i, n == SIDE - 1))
+            def _(i=i):
+                combine(0, i, 1, 512 * (i + 1), sb, mb)
+
+        out_copy(0, now, 0).start()
+        return carry
+
+    lax.fori_loop(0, SIDE, unit0, 0)
+    out_copy(0, x, 1).start()
+
+    def drain(copy):
+        copy.wait_send()
 
     for f in range(2):
         for k in ORDER:
             kv1(f, k).wait_send()
-            for j in range(SIDE):
-                kv2(f, j, k).wait_send()
             for half in range(2):
                 q_copy(f, k, half).wait_send()
+        for j in range(SIDE):
+            gather(f, j, drain)
     for f, ks in ((0, (1,)), (1, ORDER)):
 
         @pl.when(holds[f])
-        def _():
+        def _(f=f, ks=ks):
             for k in ks:
                 cache_copy(f, k).wait_send()
 
@@ -396,11 +463,12 @@
     )
     bf16 = jnp.bfloat16
     anywhere = pl.BlockSpec(memory_space=pl.ANY)
+    far = pl.BlockSpec(memory_space=pltpu.HBM)
     vmem = pl.BlockSpec(memory_space=pltpu.VMEM)
     result = pl.pallas_call(
         functools.partial(kernel, sections),
         out_shape=jax.ShapeDtypeStruct((ROWS, 64 * HEAD), bf16),
-        in_specs=[pl.BlockSpec(memory_space=pltpu.SMEM), anywhere, anywhere, anywhere, vmem, vmem],
+        in_specs=[pl.BlockSpec(memory_space=pltpu.SMEM), far, far, far, vmem, vmem],
         out_specs=anywhere,
         scratch_shapes=[
             pltpu.VMEM((2, SIDE * SIDE, ROWS, 2 * HEAD), bf16),
@@ -428,7 +496,7 @@
         compiler_params=pltpu.CompilerParams(
             collective_id=0, has_side_effects=True, vmem_limit_bytes=48 << 20
         ),
-    )(lengths, query[0], keyval[0], cache[0, 0], block_tab, row_tab)
+    )(lengths, *(pltpu.with_memory_space_constraint(z, pltpu.HBM) for z in (query[0], keyval[0], cache[0, 0])), block_tab, row_tab)
     return result[None]
 
 

time: 79.6 us -> 72.1 us (0.906)
  the two profiles are of different devices: /device:TPU:30 before, /device:TPU:5 now
where the time goes in v2:
time: 72.1 us; the launch traced here: 71.9 us
  Pallas kernels  68.6 us (95%)
  between operations  1.35 us (2%)
  local copies, waits for them, and re-layouts  1.32 us (2%)
    pallas_call x1, Pallas kernels, on_device(): pl.pallas_call(functools.partial(kernel, sections), out_shape=jax.ShapeDt...  68.6 us

profile of v2, /device:TPU:5, one launch (start us, length us, event | category | flops | bytes accessed | tf_op | source)
XLA Modules:
  0.0 71.9 jit_solution(5780441411758036232)
XLA Ops:
  1.3 0.1 multiply_cosine_fusion.1
  1.5 0.1 maximum_bitcast_fusion.2
  1.5 0.3 multiply_cosine_fusion
  1.9 0.1 maximum_bitcast_fusion
  2.0 68.6 %shard_map.55 = bf16[128,8192]{1,0:T(8,128)(2,1)S(1)} custom-call(s32[1]{0:T(128)S(6)} %copy.8.length_ref, bf16[128,8192]{1,0:T(8,128)(2,1)} %bitcast.21, bf16[128,2048]{1,0:T(8,128)(2,1)} %bitcast.22, bf16[256,256]{1,0:T(8,128)(2,1)} %bitcast.23, f32[4,16,1,128]{3,2,1,0:T(1,128)S(1)} %bitcast.20, f32[2,128,128]{2,1,0:T(8,128)S(1)} %pad_maximum_fusion.row_tab), custom_call_target="tpu_custom_call" | custom-call | tf_op jit(solution)/shard_map/pallas_call | solution.py:468
  70.6 1.3 %copy.9 = bf16[1,128,8192]{2,1,0:T(8,128)(2,1)} copy(bf16[1,128,8192]{2,1,0:T(8,128)(2,1)S(1)} %bitcast.19) | data formatting | bytes 4194304
  (5 shorter events, 0.0 us)

commit v3 on v2

--- a/solution.py
+++ b/solution.py
@@ -19,7 +19,7 @@
 SCALE = math.log2(math.e) / math.sqrt(HEAD)
 MESH = pl.DeviceIdType.MESH
 CONTRACT = (((1,), (1,)), ((), ()))
-ORDER = (1, 3, 2)
+ORDER = (2, 1, 3)
 
 
 def place(family, a, t):
@@ -169,7 +169,11 @@
     def gather(f, j, act):
         for k in ORDER:
             if f == 0:
-                act(kv2(f, j, k))
+
+                @pl.when(jnp.logical_or(lax.rem(x + j, SIDE) < SIDE - 1, y + k < SIDE))
+                def _(k=k):
+                    act(kv2(f, j, k))
+
             else:
 
                 @pl.when(row_at[f] + k < SIDE)
@@ -197,6 +201,9 @@
             cache_copy(1, k).start()
 
     values[:, :, HEAD:] = jnp.ones((2, CACHE + SPAN, HEAD), jnp.bfloat16)
+    last = CACHE + SPAN - 512
+    values[0, last:, :HEAD] = jnp.zeros((512, HEAD), jnp.bfloat16)
+    keys[0, last:, :] = jnp.zeros((512, HEAD), jnp.bfloat16)
 
     def forward(f):
         for j in ORDER:
@@ -358,13 +365,22 @@
 
     def take_piece(a, carry):
         for k in ORDER:
-            kv_wait(0, place(0, a, lax.rem(row_at[0] + k, SIDE)))
+
+            @pl.when(jnp.logical_or(a < SIDE - 1, y + k >= SIDE))
+            def _(k=k):
+                kv_wait(0, place(0, a, lax.rem(y + k, SIDE)))
+
         for t in range(SIDE):
-            take_block(0, place(0, a, t))
+
+            @pl.when(jnp.logical_or(a < SIDE - 1, t <= y))
+            def _(t=t):
+                take_block(0, place(0, a, t))
+
         return carry
 
-    lax.fori_loop(0, SIDE, take_piece, 0)
-    take_query(0, lax.rem(x + 1, SIDE), 0, qa)
+    first = lax.rem(x + 1, SIDE)
+    lax.fori_loop(0, first + 1, take_piece, 0)
+    take_query(0, first, 0, qa)
     for i in range(SIDE):
 
         @pl.when(lax.rem(x + 1, SIDE) == i)
@@ -377,10 +393,6 @@
         now = lax.rem(x + 1 + n, SIDE)
         then = lax.rem(now + 1, SIDE)
         take_query(0, now, 1, qb)
-
-        @pl.when(n < SIDE - 1)
-        def _():
-            take_query(0, then, 0, qa)
 
         for i in range(SIDE):
 
@@ -389,6 +401,14 @@
                 reach = 512 * (i + 1)
                 score(0, qb, reach, shift, sb, mb)
                 combine(0, i, 0, reach, sa, ma)
+
+        @pl.when(jnp.logical_and(n < SIDE - 1, then > first))
+        def _():
+            take_piece(then, 0)
+
+        @pl.when(n < SIDE - 1)
+        def _():
+            take_query(0, then, 0, qa)
 
         @pl.when(n > 0)
         def _():

time: 72.1 us -> 70.5 us (0.978)
  Pallas kernels: 68.6 us -> 67 us
    pallas_call x1, Pallas kernels: 68.6 us -> 67 us  [on_device(): pl.pallas_call(functools.partial(kernel, sections), out_shape=jax.ShapeDt...]
where the time goes in v3:
time: 70.5 us; the launch traced here: 70.3 us
  Pallas kernels  67 us (95%)
  between operations  1.35 us (2%)
  local copies, waits for them, and re-layouts  1.32 us (2%)
    pallas_call x1, Pallas kernels, on_device(): pl.pallas_call(functools.partial(kernel, sections), out_shape=jax.ShapeDt...  67 us

profile of v3, /device:TPU:5, one launch (start us, length us, event | category | flops | bytes accessed | tf_op | source)
XLA Modules:
  0.0 70.3 jit_solution(3253217008518556377)
XLA Ops:
  1.3 0.1 multiply_cosine_fusion.1
  1.5 0.1 maximum_bitcast_fusion.2
  1.5 0.3 multiply_cosine_fusion
  1.9 0.1 maximum_bitcast_fusion
  2.0 67.0 %shard_map.55 = bf16[128,8192]{1,0:T(8,128)(2,1)S(1)} custom-call(s32[1]{0:T(128)S(6)} %copy.8.length_ref, bf16[128,8192]{1,0:T(8,128)(2,1)} %bitcast.21, bf16[128,2048]{1,0:T(8,128)(2,1)} %bitcast.22, bf16[256,256]{1,0:T(8,128)(2,1)} %bitcast.23, f32[4,16,1,128]{3,2,1,0:T(1,128)S(1)} %bitcast.20, f32[2,128,128]{2,1,0:T(8,128)S(1)} %pad_maximum_fusion.row_tab), custom_call_target="tpu_custom_call" | custom-call | tf_op jit(solution)/shard_map/pallas_call | solution.py:488
  69.0 1.3 %copy.9 = bf16[1,128,8192]{2,1,0:T(8,128)(2,1)} copy(bf16[1,128,8192]{2,1,0:T(8,128)(2,1)S(1)} %bitcast.19) | data formatting | bytes 4194304
  (5 shorter events, 0.0 us)
